TPU v7x, 128 devices: a whole 4x4x4 slice. The times are simulated.
128 devices in a mesh: space: 16 (over y, x), vel: 8 (over z, core).
Axes of the slice: x: 4, y: 4, z: 4, core: 2. Of those that a mesh axis runs over, the one named last changes fastest.
Arguments:
- space_factor: float32 [32, 64, 16, 128], P(None, 'space'), may hold values from -16 to 16
- core_matrix: float32 [32, 32], replicated, may hold values from -0.5 to 3
- velocity_factor: float32 [32, 110592], P(None, 'vel'), may hold values from -5 to 5
- collision_rates: float32 [64, 16, 128], P('space'), may hold values from 0.05 to 0.5
Outputs:
- space_next: float32 [32, 64, 16, 128], P(None, 'space')
- core_next: float32 [32, 32], replicated
- velocity_next: float32 [32, 110592], P(None, 'vel')
All inputs are finite; a program needn't handle non-finite values.
Results may differ from a plain program's by a relative error of at most 0.0003.
Values sent between devices are 32-bit elements; how exact they have to be, the bound alone decides.
No kernel may reach another device: no remote copies, remote signals or barrier semaphores. Data moves between devices by JAX's collectives and lax.ppermute only.
A program may use at most 128 MiB of HBM per device.

v0:
```python
import jax
import jax.numpy as jnp
from jax import lax
from jax.sharding import PartitionSpec as P

NVD = 48
SUB = 3
highest = lax.Precision.HIGHEST
velocity_extent = 0.25
thermal_speed = 0.125
time_step = 1.0


def from_behind(block, axis, distance):
    devices = range(lax.axis_size(axis))
    route = [((i - distance) % len(devices), i) for i in devices]
    return lax.ppermute(block, axis, route)


def padded_2(cells, sides, width):
    for axis, dim in sides:
        count = lax.axis_size(axis)
        head = lax.slice_in_dim(cells, 0, width, axis=dim)
        tail = lax.slice_in_dim(cells, cells.shape[dim] - width, cells.shape[dim], axis=dim)
        cells = jnp.concatenate(
            [
                lax.ppermute(tail, axis, [(i, (i + 1) % count) for i in range(count)]),
                cells,
                lax.ppermute(head, axis, [((i + 1) % count, i) for i in range(count)]),
            ],
            axis=dim,
        )
    return cells


def velocity_grid(first_point, length):
    points = first_point + jnp.arange(length, dtype=jnp.int32)
    digits = [points // (NVD * NVD), points // NVD % NVD, points % NVD]
    components = [
        velocity_extent * ((2 * numeral + 1).astype(jnp.float32) / NVD - 1.0) for numeral in digits
    ]
    axis_points = velocity_extent * (
        (2 * jnp.arange(NVD, dtype=jnp.int32) + 1).astype(jnp.float32) / NVD - 1.0
    )
    twice_variance = 2.0 * thermal_speed * thermal_speed
    line_mean = jnp.mean(jnp.exp(-axis_points * axis_points / twice_variance))
    squared_speed = (
        components[0] * components[0]
        + components[1] * components[1]
        + components[2] * components[2]
    )
    profile = jnp.exp(-squared_speed / twice_variance) / (line_mean * line_mean * line_mean)
    return (jnp.stack(components), profile)


def products(leading, others, divisor):
    return lax.dot_general(leading, others, (((1,), (1,)), ((), ())), precision=highest) / divisor


def flatten_rows(values):
    return values.reshape(values.shape[0], -1)


def apply_rows(matrix, values):
    return jnp.dot(matrix, flatten_rows(values), precision=highest).reshape(
        (matrix.shape[0],) + values.shape[1:]
    )


def triangular_inverse(gram_matrix):
    factor = jnp.linalg.cholesky(gram_matrix)
    identity = jnp.eye(gram_matrix.shape[0], dtype=gram_matrix.dtype)
    return jax.scipy.linalg.solve_triangular(factor, identity, lower=True)


def lower_differences(values, lower_plane):
    shifted = jnp.concatenate([lower_plane, values[:, :-1]], axis=1)
    return [values - shifted, values - jnp.roll(values, 1, 2), values - jnp.roll(values, 1, 3)]


def velocity_stack(values, velocity):
    positive = jnp.maximum(velocity, 0.0)
    negative = jnp.minimum(velocity, 0.0)
    rank_count = values.shape[0]
    forward = (values[None] * positive[:, None]).reshape(3 * rank_count, -1)
    backward = (values[None] * negative[:, None]).reshape(3 * rank_count, -1)
    return jnp.concatenate([forward, backward], axis=0)


def mixing(space_terms):
    rank_count = space_terms.shape[0]
    backward = [
        space_terms[:, dimension * rank_count : (dimension + 1) * rank_count]
        for dimension in range(3)
    ]
    forward = [-section.T for section in backward]
    return jnp.concatenate(
        backward + forward + [space_terms[:, 3 * rank_count : 4 * rank_count]], axis=1
    )


def kinetic_update(padded, rates, flux_blocks, weights, moments):
    center = padded[:, 1:-1]
    backward = [
        center - padded[:, :-2],
        center - jnp.roll(center, 1, 2),
        center - jnp.roll(center, 1, 3),
    ]
    forward = [
        padded[:, 2:] - center,
        jnp.roll(center, -1, 2) - center,
        jnp.roll(center, -1, 3) - center,
    ]
    stacked = jnp.concatenate(backward + forward, axis=0).reshape(6 * center.shape[0], -1)
    flat_center = flatten_rows(center)
    transport = jnp.dot(flux_blocks, stacked, precision=highest)
    density = jnp.dot(weights, flat_center, precision=highest)
    change = -transport + rates.reshape(1, -1) * (moments[:, None] * density[None, :] - flat_center)
    return (flat_center + time_step * change).reshape(center.shape)


def velocity_update(values, mixing_blocks, velocity, profile, column_means):
    rank_count = values.shape[0]
    stacked = jnp.concatenate([velocity_stack(values, velocity), values], axis=0)
    change = -jnp.dot(mixing_blocks, stacked, precision=highest)
    source = jnp.dot(mixing_blocks[:, 6 * rank_count :], column_means, precision=highest)
    return values + time_step * (change + source[:, None] * profile[None, :])


def core_update(current, space_terms, point_terms, weights, moments):
    rank_count = current.shape[0]
    scaled = jnp.dot(space_terms[:, 3 * rank_count : 4 * rank_count], current, precision=highest)
    change = -scaled + jnp.outer(jnp.dot(scaled, weights, precision=highest), moments)
    for dimension in range(3):
        section = space_terms[:, dimension * rank_count : (dimension + 1) * rank_count]
        plus_block = point_terms[:, dimension * rank_count : (dimension + 1) * rank_count]
        minus_block = point_terms[:, (dimension + 3) * rank_count : (dimension + 4) * rank_count]
        change = change - jnp.dot(
            jnp.dot(section, current, precision=highest), plus_block.T, precision=highest
        )
        change = change + jnp.dot(
            jnp.dot(section.T, current, precision=highest), minus_block.T, precision=highest
        )
    return current + time_step * change


def cell_share(values):
    merged = values.reshape(values.shape[0], values.shape[1] * values.shape[2], values.shape[3])
    return flatten_rows(merged)


def combine(space_part, point_part):
    space_total = lax.psum(space_part, "space")
    point_total = lax.psum(point_part, "vel")
    return (space_total, point_total)


def project(
    space_state,
    lower_plane,
    space_old,
    rates,
    point_state,
    point_old,
    velocity,
    profile,
    cells_total,
    points_total,
):
    rank_count = space_state.shape[0]
    share_profile = profile[None]
    ones_row = jnp.ones_like(share_profile)
    space_part = products(cell_share(space_state), cell_share(space_state), cells_total)
    point_part = products(
        point_state, jnp.concatenate([point_state, ones_row, share_profile], axis=0), points_total
    )
    space_sums, point_sums = combine(space_part, point_part)
    space_inverse = triangular_inverse(space_sums)
    point_inverse = triangular_inverse(point_sums[:, :rank_count])
    weights = jnp.dot(point_inverse, point_sums[:, rank_count], precision=highest)
    moments = jnp.dot(point_inverse, point_sums[:, rank_count + 1], precision=highest)
    space_new = apply_rows(space_inverse, space_state)
    point_new = jnp.dot(point_inverse, point_state, precision=highest)
    new_lower = apply_rows(space_inverse, lower_plane)
    space_items = lower_differences(space_new, new_lower) + [rates[None] * space_new, space_old]
    space_others = jnp.concatenate([cell_share(member) for member in space_items], axis=0)
    space_part = products(cell_share(space_new), space_others, cells_total)
    point_others = jnp.concatenate([velocity_stack(point_new, velocity), point_old], axis=0)
    point_part = products(point_new, point_others, points_total)
    space_terms, point_terms = combine(space_part, point_part)
    return (space_new, point_new, space_terms, point_terms, weights, moments)


def per_device(space_factor, core_matrix, velocity_factor, collision_rates):
    rank_count = core_matrix.shape[0]
    point_rows = velocity_factor.shape[1]
    cells_total = (
        space_factor.shape[1]
        * space_factor.shape[2]
        * space_factor.shape[3]
        * lax.axis_size("space")
    )
    points_total = point_rows * lax.axis_size("vel")
    velocity, profile = velocity_grid(lax.axis_index("vel") * point_rows, point_rows)
    start_lower = from_behind(space_factor[:, -1:], "space", 1)
    basis_space, basis_point, space_terms, point_terms, weights, moments = project(
        space_factor,
        start_lower,
        space_factor,
        collision_rates,
        velocity_factor,
        velocity_factor,
        velocity,
        profile,
        cells_total,
        points_total,
    )
    current = jnp.dot(
        jnp.dot(space_terms[:, 4 * rank_count :], core_matrix, precision=highest),
        point_terms[:, 6 * rank_count :].T,
        precision=highest,
    )
    flux_blocks = point_terms[:, : 6 * rank_count]
    kinetic = apply_rows(current.T, basis_space)
    for substep in range(SUB):
        padded = padded_2(kinetic, (("space", 1),), 1)
        kinetic = kinetic_update(padded, collision_rates, flux_blocks, weights, moments)
    lower_plane = from_behind(kinetic[:, -1:], "space", 1)
    mixing_blocks = mixing(space_terms)
    spread_point = jnp.dot(current, basis_point, precision=highest)
    for substep in range(SUB):
        local_total = jnp.sum(spread_point, axis=1) / points_total
        column_means = lax.psum(local_total, "vel")
        spread_point = velocity_update(spread_point, mixing_blocks, velocity, profile, column_means)
    fresh_space, fresh_point, space_terms, point_terms, weights, moments = project(
        kinetic,
        lower_plane,
        basis_space,
        collision_rates,
        spread_point,
        basis_point,
        velocity,
        profile,
        cells_total,
        points_total,
    )
    current = jnp.dot(
        jnp.dot(space_terms[:, 4 * rank_count :], current, precision=highest),
        point_terms[:, 6 * rank_count :].T,
        precision=highest,
    )
    for substep in range(SUB):
        current = core_update(current, space_terms, point_terms, weights, moments)
    return (fresh_space, current, fresh_point)


def solution(mesh):
    return jax.shard_map(
        per_device,
        mesh=mesh,
        in_specs=(P(None, "space", None, None), P(), P(None, "vel"), P("space", None, None)),
        out_specs=(P(None, "space", None, None), P(), P(None, "vel")),
        check_vma=False,
    )
```

profile of v0, /device:TPU:96, one launch (start us, length us, event | category | flops | bytes accessed | tf_op | source)
XLA Modules:
  0.0 670.9 jit_solution(7387218225295782337)
XLA Ops:
  3.8 3.7 fusion.63
  7.5 73.3 %psum.77 = f32[32,32]{0,1:T(8,128)S(1)} all-reduce(f32[32,32]{0,1:T(8,128)S(1)} %fusion.63), channel_id=1, replica_groups=mesh['space'=16,'vel'=8] {'space'}, use_global_device_ids=true, to_apply=%region_0.1 | all-reduce | flops 1024 | bytes 8192 | tf_op jit(solution)/shard_map/psum | solution.py:153
  80.8 2.9 cholesky.74
  85.1 2.4 custom-call.8
  87.8 2.8 fusion.72
  97.8 4.1 fusion.59
  101.9 19.6 %psum.79 = f32[32,34]{0,1:T(8,128)S(1)} all-reduce(f32[32,34]{0,1:T(8,128)S(1)} %fusion.59), channel_id=1, replica_groups=mesh['space'=16,'vel'=8] {'vel'}, use_global_device_ids=true, to_apply=%region_5.8 | all-reduce | flops 1088 | bytes 8704 | tf_op jit(solution)/shard_map/psum | solution.py:154
  121.7 2.9 cholesky.85
  125.9 2.4 custom-call.9
  128.6 3.2 fusion.292
  135.9 11.1 %fusion.54 = f32[32,224]{1,0:T(8,128)S(1)} fusion(f32[32,13824]{1,0:T(8,128)S(1)} %fusion.292, f32[32,13824]{1,0:T(8,128)S(1)} %copy-done.16, f32[96,13824]{1,0:T(8,128)S(1)} %bitcast.366, f32[96,13824]{1,0:T(8,128)S(1)} %bitcast.365), kind=kOutput, calls=%fused_computation.74 | convolution fusion | flops 1195285504 | bytes 14184448 | tf_op jit(solution)/shard_map/dot_general | solution.py:57
  149.3 23.7 %psum.80 = f32[32,224]{1,0:T(8,128)S(1)} all-reduce(f32[32,224]{1,0:T(8,128)S(1)} %fusion.54), channel_id=1, replica_groups=mesh['space'=16,'vel'=8] {'vel'}, use_global_device_ids=true, to_apply=%region_6.9 | all-reduce | flops 7168 | bytes 57344 | tf_op jit(solution)/shard_map/psum | solution.py:154
  177.4 1.9 fusion.70
  180.6 5.0 convolution_multiply_fusion.1
  185.6 69.8 %psum.78 = f32[32,160]{1,0:T(8,128)S(1)} all-reduce(f32[32,160]{1,0:T(8,128)S(1)} %convolution_multiply_fusion.1), channel_id=1, replica_groups=mesh['space'=16,'vel'=8] {'space'}, use_global_device_ids=true, to_apply=%region_3.6 | all-reduce | flops 5120 | bytes 40960 | tf_op jit(solution)/shard_map/psum | solution.py:153
  256.4 2.9 fusion.289
  267.3 13.0 %psum.83 = f32[32]{0:T(128)S(1)} all-reduce(f32[32]{0:T(128)S(1)} %broadcast_multiply_fusion.12), channel_id=1, replica_groups=mesh['space'=16,'vel'=8] {'vel'}, use_global_device_ids=true, to_apply=%region_10.13 | all-reduce | flops 32 | bytes 256 | tf_op jit(solution)/shard_map/psum | solution.py:233
  280.5 6.7 %broadcast_multiply_fusion.7 = (f32[3,32,13824]{2,1,0:T(8,128)}, f32[3,32,13824]{2,1,0:T(8,128)}) fusion(f32[32,13824]{1,0:T(8,128)} %get-tuple-element.52, f32[3,13824]{1,0:T(4,128)S(1)} %get-tuple-element.45, f32[3,13824]{1,0:T(4,128)} %copy-done.7), kind=kLoop, calls=%fused_computation.60 | loop fusion | flops 2654208 | bytes 12718080 | tf_op jit(solution)/shard_map/mul | solution.py:85
  288.0 10.7 %fusion.290 = (f32[32]{0:T(128)S(1)}, f32[32,13824]{1,0:T(8,128)S(1)}) fusion(f32[32,13824]{1,0:T(8,128)} %get-tuple-element.52, f32[13824]{0:T(1024)} %fusion.118, f32[32]{0:T(128)S(1)} %convolution_bitcast_fusion.10, f32[32,224]{1,0:T(8,128)} %concatenate.176, f32[96,13824]{1,0:T(8,128)} %bitcast.358, f32[96,13824]{1,0:T(8,128)} %bitcast.357), kind=kOutput, calls=%fused_computation.412 | convolution fusion | flops 1197490176 | bytes 14240000 | tf_op jit(solution)/shard_map/dot_general | solution.py:125
  298.7 5.2 broadcast_multiply_fusion.5
  303.9 12.4 %psum.84 = f32[32]{0:T(128)S(1)} all-reduce(f32[32]{0:T(128)S(1)} %broadcast_multiply_fusion.11), channel_id=1, replica_groups=mesh['space'=16,'vel'=8] {'vel'}, use_global_device_ids=true, to_apply=%region_12.15 | all-reduce | flops 32 | bytes 256 | tf_op jit(solution)/shard_map/psum | solution.py:233
  316.5 11.5 %fusion.291 = (f32[32]{0:T(128)S(1)}, f32[32,13824]{1,0:T(8,128)}) fusion(f32[32,13824]{1,0:T(8,128)} %copy-done.19, f32[13824]{0:T(1024)S(1)} %copy-done.30, f32[32]{0:T(128)S(1)} %convolution_bitcast_fusion.9, f32[32,224]{1,0:T(8,128)} %concatenate.176, f32[96,13824]{1,0:T(8,128)} %bitcast.360, f32[96,13824]{1,0:T(8,128)} %bitcast.359), kind=kOutput, calls=%fused_computation.413 | convolution fusion | flops 1197490176 | bytes 14240000 | tf_op jit(solution)/shard_map/dot_general | solution.py:125
  328.0 12.8 %psum.85 = f32[32]{0:T(128)S(1)} all-reduce(f32[32]{0:T(128)S(1)} %broadcast_multiply_fusion.10), channel_id=1, replica_groups=mesh['space'=16,'vel'=8] {'vel'}, use_global_device_ids=true, to_apply=%region_14.17 | all-reduce | flops 32 | bytes 256 | tf_op jit(solution)/shard_map/psum | solution.py:233
  341.0 2.8 broadcast_multiply_fusion.3
  343.9 7.3 %fusion.1 = f32[32,13824]{1,0:T(8,128)S(1)} fusion(f32[32,13824]{1,0:T(8,128)S(1)} %copy-done.18, f32[32,224]{1,0:T(8,128)S(1)} %copy-done.33, f32[96,13824]{1,0:T(8,128)S(1)} %bitcast.364, f32[96,13824]{1,0:T(8,128)S(1)} %bitcast.363, f32[32]{0:T(128)S(1)} %convolution_bitcast_fusion.8, f32[13824]{0:T(1024)S(1)} %copy-done.30), kind=kOutput, calls=%fused_computation.2 | convolution fusion | flops 1197047808 | bytes 14239872 | tf_op jit(solution)/shard_map/dot_general | solution.py:125
  352.4 2.0 fusion.57
  354.4 23.2 %psum.86 = f32[32,34]{0,1:T(8,128)S(1)} all-reduce(f32[32,34]{0,1:T(8,128)S(1)} %fusion.57), channel_id=1, replica_groups=mesh['space'=16,'vel'=8] {'vel'}, use_global_device_ids=true, to_apply=%region_15.18 | all-reduce | flops 1088 | bytes 8704 | tf_op jit(solution)/shard_map/psum | solution.py:154
  377.7 2.9 cholesky.107
  382.0 2.4 custom-call.11
  384.7 3.1 fusion.298
  388.0 2.5 broadcast_multiply_fusion.1
  390.6 10.9 %fusion.51 = f32[32,224]{1,0:T(8,128)S(1)} fusion(f32[32,13824]{1,0:T(8,128)S(1)} %fusion.298, f32[32,13824]{1,0:T(8,128)S(1)} %copy-done.5, f32[96,13824]{1,0:T(8,128)S(1)} %bitcast.362, f32[96,13824]{1,0:T(8,128)S(1)} %bitcast.361), kind=kOutput, calls=%fused_computation.73 | convolution fusion | flops 1195285504 | bytes 14184448 | tf_op jit(solution)/shard_map/dot_general | solution.py:57
  401.6 23.6 %psum.87 = f32[32,224]{1,0:T(8,128)S(1)} all-reduce(f32[32,224]{1,0:T(8,128)S(1)} %fusion.51), channel_id=1, replica_groups=mesh['space'=16,'vel'=8] {'vel'}, use_global_device_ids=true, to_apply=%region_16.19 | all-reduce | flops 7168 | bytes 57344 | tf_op jit(solution)/shard_map/psum | solution.py:154
  425.2 5.6 collective-permute-start.2
  434.5 3.1 collective-permute-done.2
  438.4 7.3 %fusion.38 = f32[32,8192]{1,0:T(8,128)S(1)} fusion(f32[32,8192]{1,0:T(8,128)S(1)} %fusion.293, f32[24,8,64,128]{3,2,1,0:T(8,128)S(1)} %bitcast.354, f32[8192]{0:T(1024)S(1)} %bitcast.381, f32[32]{0:T(128)S(1)} %copy-done.34, f32[8192]{0:T(1024)S(1)} %bitcast.375, f32[32,224]{1,0:T(8,128)S(1)} %psum.80), kind=kOutput, calls=%fused_computation.44 | convolution fusion | flops 605552640 | bytes 8482944 | tf_op jit(solution)/shard_map/dot_general | solution.py:116
  447.2 6.2 collective-permute-start.4
  454.0 5.4 collective-permute-done.3
  460.8 7.3 %fusion.36 = f32[32,8192]{1,0:T(8,128)S(1)} fusion(f32[32,8192]{1,0:T(8,128)S(1)} %fusion.38, f32[24,8,64,128]{3,2,1,0:T(8,128)S(1)} %bitcast.355, f32[8192]{0:T(1024)S(1)} %bitcast.382, f32[32]{0:T(128)S(1)} %copy-done.34, f32[8192]{0:T(1024)S(1)} %bitcast.376, f32[32,224]{1,0:T(8,128)S(1)} %psum.80), kind=kOutput, calls=%fused_computation.41 | convolution fusion | flops 605552640 | bytes 8482944 | tf_op jit(solution)/shard_map/dot_general | solution.py:116
  469.6 5.6 collective-permute-start.6
  475.8 4.8 collective-permute-done.5
  482.0 7.2 %fusion.34 = f32[32,8192]{1,0:T(8,128)S(1)} fusion(f32[32,8192]{1,0:T(8,128)S(1)} %fusion.36, f32[24,8,64,128]{3,2,1,0:T(8,128)S(1)} %bitcast.356, f32[8192]{0:T(1024)S(1)} %bitcast.380, f32[32]{0:T(128)S(1)} %copy-done.34, f32[8192]{0:T(1024)S(1)} %bitcast.377, f32[32,224]{1,0:T(8,128)S(1)} %psum.80), kind=kOutput, calls=%fused_computation.38 | convolution fusion | flops 605552640 | bytes 8482944 | tf_op jit(solution)/shard_map/dot_general | solution.py:116
  490.3 74.4 %psum.81 = f32[32,32]{0,1:T(8,128)S(1)} all-reduce(f32[32,32]{0,1:T(8,128)S(1)} %convolution_multiply_fusion.2), channel_id=1, replica_groups=mesh['space'=16,'vel'=8] {'space'}, use_global_device_ids=true, to_apply=%region_7.10 | all-reduce | flops 1024 | bytes 8192 | tf_op jit(solution)/shard_map/psum | solution.py:153
  564.7 2.9 cholesky.96
  569.0 2.4 custom-call.10
  574.2 9.2 %collective-permute-done.7 = f32[32,1,16,128]{3,2,1,0:T(8,128)S(1)} collective-permute-done((f32[32,1,16,128]{3,2,1,0:T(8,128)S(1)}, f32[32,1,16,128]{3,2,1,0:T(8,128)S(1)}, u32[]{:S(2)}, u32[]{:S(2)}) %collective-permute-start.7) | collective-permute-done | bytes 262176 | tf_op jit(solution)/shard_map/ppermute | solution.py:17
  586.4 4.9 convolution_multiply_fusion
  591.3 69.5 %psum.82 = f32[32,160]{1,0:T(8,128)S(1)} all-reduce(f32[32,160]{1,0:T(8,128)S(1)} %convolution_multiply_fusion), channel_id=1, replica_groups=mesh['space'=16,'vel'=8] {'space'}, use_global_device_ids=true, to_apply=%region_8.11 | all-reduce | flops 5120 | bytes 40960 | tf_op jit(solution)/shard_map/psum | solution.py:153
  (254 shorter events, 66.2 us)
Async XLA Ops:
  0.6 255.4 %copy-start = (f32[32,32]{1,0:T(8,128)S(1)}, f32[32,32]{1,0:T(8,128)}, u32[]{:S(2)}) copy-start(f32[32,32]{1,0:T(8,128)} %param.8) | copy-start | bytes 12292
  2.3 171.5 %collective-permute-start = (f32[32,1,16,128]{3,2,1,0:T(8,128)}, f32[32,1,16,128]{3,2,1,0:T(8,128)}, u32[]{:S(2)}, u32[]{:S(2)}) collective-permute-start(f32[32,1,16,128]{3,2,1,0:T(8,128)} %slice.264), channel_id=1, source_target_pairs={{120,0},{0,8},{8,16},{16,24},{24,32},{32,40},{40,48},{48,56},{56,6... | collective-permute-start | bytes 786440 | tf_op jit(solution)/shard_map/ppermute | solution.py:17
  87.8 3.0 copy-start.26
  97.2 0.6 copy-start.31
  97.8 36.3 %copy-start.36 = (f32[34]{0:T(128)}, f32[34]{0:T(128)S(1)}, u32[]{:S(2)}) copy-start(f32[34]{0:T(128)S(1)} %pad.64.clone) | copy-start | bytes 412
  121.6 12.6 %copy-start.25 = (f32[32,34]{0,1:T(8,128)}, f32[32,34]{0,1:T(8,128)S(1)}, u32[]{:S(2)}) copy-start(f32[32,34]{0,1:T(8,128)S(1)} %psum.79) | copy-start | bytes 13060
  128.3 5.4 copy-start.10
  131.8 3.8 copy-start.3
  134.3 1.2 copy-start.7
  134.3 1.6 copy-start.16
  135.9 38.0 %copy-start.27 = (f32[32,32]{1,0:T(8,128)S(1)}, f32[32,32]{1,0:T(8,128)}, u32[]{:S(2)}) copy-start(f32[32,32]{1,0:T(8,128)} %copy-done.26) | copy-start | bytes 12292
  175.4 4.5 copy-start.22
  176.7 3.3 copy-start.6
  179.9 76.5 %copy-start.4 = (f32[32,13824]{1,0:T(8,128)S(1)}, f32[32,13824]{1,0:T(8,128)}, u32[]{:S(2)}) copy-start(f32[32,13824]{1,0:T(8,128)} %copy-done.3) | copy-start | bytes 5308420
  255.4 24.9 %copy-start.20 = (f32[32,160]{1,0:T(8,128)}, f32[32,160]{1,0:T(8,128)S(1)}, u32[]{:S(2)}) copy-start(f32[32,160]{1,0:T(8,128)S(1)} %psum.78) | copy-start | bytes 61444
  263.0 4.2 copy-start.29
  280.5 6.8 %slice-start = ((f32[32,160]{1,0:T(8,128)}), f32[32,96]{1,0:T(8,128)S(1)}, s32[]{:S(2)}) async-start(f32[32,160]{1,0:T(8,128)} %copy-done.20), calls=%async_computation | async-start | bytes 32768 | tf_op jit(solution)/shard_map/slice | solution.py:93
  280.5 6.8 %copy-start.28 = (f32[32,32]{1,0:T(8,128)S(1)}, f32[32,32]{1,0:T(8,128)}, u32[]{:S(2)}) copy-start(f32[32,32]{1,0:T(8,128)} %get-tuple-element.47) | copy-start | bytes 12292
  287.9 10.7 %copy-start.8 = (f32[3,13824]{1,0:T(4,128)S(1)}, f32[3,13824]{1,0:T(4,128)}, u32[]{:S(2)}) copy-start(f32[3,13824]{1,0:T(4,128)} %copy-done.7) | copy-start | bytes 497668
  298.6 5.2 copy-start.19
  298.6 17.6 %copy-start.21 = (f32[32,160]{1,0:T(8,128)S(1)}, f32[32,160]{1,0:T(8,128)}, u32[]{:S(2)}) copy-start(f32[32,160]{1,0:T(8,128)} %copy-done.20) | copy-start | bytes 61444
  298.7 17.8 %copy-start.30 = (f32[13824]{0:T(1024)S(1)}, f32[13824]{0:T(1024)}, u32[]{:S(2)}) copy-start(f32[13824]{0:T(1024)} %fusion.118) | copy-start | bytes 165892
  341.0 2.8 copy-start.18
  341.0 2.8 copy-start.33
  343.8 8.6 %copy-start.32 = (f32[1,13824]{1,0:T(1,128)S(1)}, f32[1,13824]{1,0:T(1,128)}, u32[]{:S(2)}) copy-start(f32[1,13824]{1,0:T(1,128)} %copy-done.31) | copy-start | bytes 165892
  343.8 8.6 %copy-start.37 = (f32[34]{0:T(128)S(1)}, f32[34]{0:T(128)}, u32[]{:S(2)}) copy-start(f32[34]{0:T(128)} %copy-done.36) | copy-start | bytes 412
  351.2 1.2 copy-start.17
  387.7 2.9 copy-start.9
  388.0 2.6 copy-start.5
  390.5 40.9 %collective-permute-start.1 = (f32[32,1,16,128]{3,2,1,0:T(8,128)}, f32[32,1,16,128]{3,2,1,0:T(8,128)}, u32[]{:S(2)}, u32[]{:S(2)}) collective-permute-start(f32[32,1,16,128]{3,2,1,0:T(8,128)} %get-tuple-element.44), channel_id=1, source_target_pairs={{0,8},{8,16},{16,24},{24,32},{32,40},{40,48},{48,56},{56,64},{64,7... | collective-permute-start | bytes 786440 | tf_op jit(solution)/shard_map/ppermute | solution.py:27
  390.6 40.2 %copy-start.35 = (f32[32,1]{0,1:T(1,128)S(1)}, f32[32,1]{0,1:T(1,128)}, u32[]{:S(2)}) copy-start(f32[32,1]{0,1:T(1,128)} %convolution_bitcast_fusion.11) | copy-start | bytes 388
  390.6 41.9 %copy-start.24 = (f32[32,4,1,128]{3,2,1,0:T(1,128)S(1)}, f32[32,4,1,128]{3,2,1,0:T(1,128)}, u32[]{:S(2)}) copy-start(f32[32,4,1,128]{3,2,1,0:T(1,128)} %get-tuple-element.42) | copy-start | bytes 196612
  425.2 8.9 %copy-start.14 = (f32[32,4,16,127]{3,2,1,0:T(8,128)S(1)}, f32[32,4,16,127]{3,2,1,0:T(8,128)}, u32[]{:S(2)}) copy-start(f32[32,4,16,127]{3,2,1,0:T(8,128)} %get-tuple-element.36) | copy-start | bytes 3121156
  425.2 8.9 %copy-start.15 = (f32[32,4,16,1]{3,2,1,0:T(8,128)S(1)}, f32[32,4,16,1]{3,2,1,0:T(8,128)}, u32[]{:S(2)}) copy-start(f32[32,4,16,1]{3,2,1,0:T(8,128)} %get-tuple-element.38) | copy-start | bytes 24580
  425.2 12.4 %collective-permute-start.2 = (f32[32,1,16,128]{3,2,1,0:T(8,128)}, f32[32,1,16,128]{3,2,1,0:T(8,128)S(1)}, u32[]{:S(2)}, u32[]{:S(2)}) collective-permute-start(f32[32,1,16,128]{3,2,1,0:T(8,128)} %get-tuple-element.43), channel_id=1, source_target_pairs={{8,0},{16,8},{24,16},{32,24},{40,32},{48,40},{56,48},{64,56},{72,6... | collective-permute-start | bytes 786440 | tf_op jit(solution)/shard_map/ppermute | solution.py:29
  432.5 5.2 copy-start.11
  432.5 5.2 copy-start.23
  434.1 3.9 copy-start.12
  434.1 3.9 copy-start.13
  434.5 3.9 copy-start.34
  447.0 12.3 %collective-permute-start.3 = (f32[32,1,16,128]{3,2,1,0:T(8,128)S(1)}, f32[32,1,16,128]{3,2,1,0:T(8,128)S(1)}, u32[]{:S(2)}, u32[]{:S(2)}) collective-permute-start(f32[32,1,16,128]{3,2,1,0:T(8,128)S(1)} %get-tuple-element.34), channel_id=1, source_target_pairs={{0,8},{8,16},{16,24},{24,32},{32,40},{40,48},{48,56},{56,64},{64,7... | collective-permute-start | bytes 786440 | tf_op jit(solution)/shard_map/ppermute | solution.py:27
  447.2 12.9 %collective-permute-start.4 = (f32[32,1,16,128]{3,2,1,0:T(8,128)S(1)}, f32[32,1,16,128]{3,2,1,0:T(8,128)S(1)}, u32[]{:S(2)}, u32[]{:S(2)}) collective-permute-start(f32[32,1,16,128]{3,2,1,0:T(8,128)S(1)} %get-tuple-element.33), channel_id=1, source_target_pairs={{8,0},{16,8},{24,16},{32,24},{40,32},{48,40},{56,48},{64,56},{72,6... | collective-permute-start | bytes 786440 | tf_op jit(solution)/shard_map/ppermute | solution.py:29
  469.4 11.1 %collective-permute-start.5 = (f32[32,1,16,128]{3,2,1,0:T(8,128)S(1)}, f32[32,1,16,128]{3,2,1,0:T(8,128)S(1)}, u32[]{:S(2)}, u32[]{:S(2)}) collective-permute-start(f32[32,1,16,128]{3,2,1,0:T(8,128)S(1)} %get-tuple-element.24), channel_id=1, source_target_pairs={{0,8},{8,16},{16,24},{24,32},{32,40},{40,48},{48,56},{56,64},{64,7... | collective-permute-start | bytes 786440 | tf_op jit(solution)/shard_map/ppermute | solution.py:27
  469.6 11.7 %collective-permute-start.6 = (f32[32,1,16,128]{3,2,1,0:T(8,128)S(1)}, f32[32,1,16,128]{3,2,1,0:T(8,128)S(1)}, u32[]{:S(2)}, u32[]{:S(2)}) collective-permute-start(f32[32,1,16,128]{3,2,1,0:T(8,128)S(1)} %get-tuple-element.23), channel_id=1, source_target_pairs={{8,0},{16,8},{24,16},{32,24},{40,32},{48,40},{56,48},{64,56},{72,6... | collective-permute-start | bytes 786440 | tf_op jit(solution)/shard_map/ppermute | solution.py:29
  572.9 1.3 copy-start.2
  573.6 9.8 %collective-permute-start.7 = (f32[32,1,16,128]{3,2,1,0:T(8,128)S(1)}, f32[32,1,16,128]{3,2,1,0:T(8,128)S(1)}, u32[]{:S(2)}, u32[]{:S(2)}) collective-permute-start(f32[32,1,16,128]{3,2,1,0:T(8,128)S(1)} %slice.379), channel_id=1, source_target_pairs={{120,0},{0,8},{8,16},{16,24},{24,32},{32,40},{40,48},{48,56},{56,6... | collective-permute-start | bytes 786440 | tf_op jit(solution)/shard_map/ppermute | solution.py:17
  586.2 84.5 %copy-start.1 = (f32[32,32]{1,0:T(8,128)S(1)}, f32[32,32]{1,0:T(8,128)}, u32[]{:S(2)}) copy-start(f32[32,32]{1,0:T(8,128)} %param.8) | copy-start | bytes 12292
where the time goes:
time: 679 us; the launch traced here: 671 us
  blocking collectives  415 us (61%)
  matrix products  126 us (19%)
  other arithmetic  65.2 us (10%)
  waiting for transfers between devices  22.5 us (3%)
  starting transfers between devices  19.1 us (3%)
  local copies, waits for them, and re-layouts  19 us (3%)
    psum x4, blocking collectives, combine(): space_total = lax.psum(space_part, 'space')  287 us
    psum x4, blocking collectives, combine(): point_total = lax.psum(point_part, 'vel')  90.2 us
    dot_general x8, matrix products, products(): lax.dot_general(leading, others, (((1,), (1,)), ((), ())), precision=high...  42.7 us
    psum x3, blocking collectives, per_device(): column_means = lax.psum(local_total, 'vel')  38.2 us
    dot_general x3, matrix products, velocity_update(): change = -jnp.dot(mixing_blocks, stacked, precision=highest)  29.5 us
    dot_general x3, matrix products, kinetic_update(): transport = jnp.dot(flux_blocks, stacked, precision=highest)  21.8 us
    mul x5, other arithmetic, velocity_stack(): forward = (values[None] * positive[:, None]).reshape(3 * rank_count, -1)  18.3 us
    ppermute x3, starting transfers between devices, padded_2(): lax.ppermute(head, axis, [((i + 1) % count, i) for i in range(count)])  17.3 us
  transfers between devices with their start and end apart: 8, of which 4 were waited for; matrix products, arithmetic and copies ran while one was open for 10% of the time, Pallas kernels for 0%

commit v1 on v0

--- a/solution.py
+++ b/solution.py
@@ -1,3 +1,4 @@
+import functools
 import jax
 import jax.numpy as jnp
 from jax import lax
@@ -9,6 +10,14 @@
 velocity_extent = 0.25
 thermal_speed = 0.125
 time_step = 1.0
+
+
+def change_results(z_in, mesh_name):
+    last = lax.all_gather(z_in, mesh_name).sum(axis=0)
+    return last
+
+
+_lift_ranges = functools.partial(change_results, mesh_name="vel")
 
 
 def from_behind(block, axis, distance):
@@ -151,7 +160,7 @@
 
 def combine(space_part, point_part):
     space_total = lax.psum(space_part, "space")
-    point_total = lax.psum(point_part, "vel")
+    point_total = _lift_ranges(point_part)
     return (space_total, point_total)
 
 

time: 679 us -> 640 us (0.943)
  blocking collectives: 415 us -> 376 us
    psum x4 -> x0, blocking collectives: 90.2 us -> none  [combine(): point_total = lax.psum(point_part, 'vel')]
    all_gather x0 -> x4, blocking collectives: none -> 55 us  [change_results(): last = lax.all_gather(z_in, mesh_name).sum(axis=0)]
  transfers between devices with their start and end apart: 8 -> 8, of which waited for: 4 -> 4; matrix products, arithmetic and copies ran while one was open for 10% -> 11% of each run, Pallas kernels for 0% -> 0%
where the time goes in v1:
time: 640 us; the launch traced here: 628 us
  blocking collectives  376 us (59%)
  matrix products  125 us (20%)
  other arithmetic  65.7 us (10%)
  waiting for transfers between devices  20.8 us (3%)
  starting transfers between devices  18.9 us (3%)
  local copies, waits for them, and re-layouts  17.5 us (3%)
    psum x4, blocking collectives, combine(): space_total = lax.psum(space_part, 'space')  287 us
    all_gather x4, blocking collectives, change_results(): last = lax.all_gather(z_in, mesh_name).sum(axis=0)  55 us
    dot_general x8, matrix products, products(): lax.dot_general(leading, others, (((1,), (1,)), ((), ())), precision=high...  42.7 us
    psum x3, blocking collectives, per_device(): column_means = lax.psum(local_total, 'vel')  34.1 us
    dot_general x3, matrix products, velocity_update(): change = -jnp.dot(mixing_blocks, stacked, precision=highest)  29.6 us
    dot_general x3, matrix products, kinetic_update(): transport = jnp.dot(flux_blocks, stacked, precision=highest)  21.8 us
    mul x5, other arithmetic, velocity_stack(): forward = (values[None] * positive[:, None]).reshape(3 * rank_count, -1)  18.3 us
    ppermute x3, starting transfers between devices, padded_2(): lax.ppermute(head, axis, [((i + 1) % count, i) for i in range(count)])  17.1 us
  transfers between devices with their start and end apart: 8, of which 4 were waited for; matrix products, arithmetic and copies ran while one was open for 11% of the time, Pallas kernels for 0%

profile of v1, /device:TPU:96, one launch (start us, length us, event | category | flops | bytes accessed | tf_op | source)
XLA Modules:
  0.0 628.1 jit_solution(18153081705300863856)
XLA Ops:
  3.8 3.7 fusion.63
  7.5 73.3 %psum.49 = f32[32,32]{0,1:T(8,128)S(1)} all-reduce(f32[32,32]{0,1:T(8,128)S(1)} %fusion.63), channel_id=1, replica_groups=mesh['space'=16,'vel'=8] {'space'}, use_global_device_ids=true, to_apply=%region_0.1 | all-reduce | flops 1024 | bytes 8192 | tf_op jit(solution)/shard_map/psum | solution.py:162
  80.8 2.9 cholesky.74
  85.1 2.4 custom-call.8
  87.8 2.8 fusion.72
  96.8 4.1 fusion.59
  101.0 13.2 %all-gather = f32[256,34]{1,0:T(8,128)S(1)} all-gather(f32[32,34]{1,0:T(8,128)S(1)} %fusion.59), channel_id=2, replica_groups=mesh['space'=16,'vel'=8] {'vel'}, dimensions={0}, use_global_device_ids=true | all-gather | bytes 39168 | tf_op jit(solution)/shard_map/all_gather | solution.py:16
  114.5 2.9 cholesky.85
  118.7 2.4 custom-call.9
  121.4 3.1 fusion.292
  130.2 11.1 %fusion.54 = f32[32,224]{1,0:T(8,128)S(1)} fusion(f32[32,13824]{1,0:T(8,128)S(1)} %fusion.292, f32[32,13824]{1,0:T(8,128)S(1)} %copy-done.17, f32[96,13824]{1,0:T(8,128)S(1)} %bitcast.380, f32[96,13824]{1,0:T(8,128)S(1)} %bitcast.379), kind=kOutput, calls=%fused_computation.74 | convolution fusion | flops 1195285504 | bytes 14184448 | tf_op jit(solution)/shard_map/dot_general | solution.py:66
  141.3 13.9 %all-gather.1 = f32[256,224]{1,0:T(8,128)} all-gather(f32[32,224]{1,0:T(8,128)S(1)} %fusion.54), channel_id=3, replica_groups=mesh['space'=16,'vel'=8] {'vel'}, dimensions={0}, use_global_device_ids=true | all-gather | bytes 258048 | tf_op jit(solution)/shard_map/all_gather | solution.py:16
  161.6 5.0 convolution_multiply_fusion.1
  166.6 69.8 %psum.50 = f32[32,160]{1,0:T(8,128)S(1)} all-reduce(f32[32,160]{1,0:T(8,128)S(1)} %convolution_multiply_fusion.1), channel_id=1, replica_groups=mesh['space'=16,'vel'=8] {'space'}, use_global_device_ids=true, to_apply=%region_3.6 | all-reduce | flops 5120 | bytes 40960 | tf_op jit(solution)/shard_map/psum | solution.py:162
  237.4 2.9 fusion.289
  244.7 1.7 fusion.283
  248.3 10.2 %psum.53 = f32[32]{0:T(128)S(1)} all-reduce(f32[32]{0:T(128)S(1)} %broadcast_multiply_fusion.12), channel_id=1, replica_groups=mesh['space'=16,'vel'=8] {'vel'}, use_global_device_ids=true, to_apply=%region_10.13 | all-reduce | flops 32 | bytes 256 | tf_op jit(solution)/shard_map/psum | solution.py:242
  258.7 6.7 %broadcast_multiply_fusion.7 = (f32[3,32,13824]{2,1,0:T(8,128)}, f32[3,32,13824]{2,1,0:T(8,128)}) fusion(f32[32,13824]{1,0:T(8,128)} %get-tuple-element.56, f32[3,13824]{1,0:T(4,128)S(1)} %get-tuple-element.49, f32[3,13824]{1,0:T(4,128)} %copy-done.7), kind=kLoop, calls=%fused_computation.60 | loop fusion | flops 2654208 | bytes 12718080 | tf_op jit(solution)/shard_map/mul | solution.py:94
  266.2 10.7 %fusion.290 = (f32[32]{0:T(128)S(1)}, f32[32,13824]{1,0:T(8,128)S(1)}) fusion(f32[32,13824]{1,0:T(8,128)} %get-tuple-element.56, f32[13824]{0:T(1024)} %fusion.118, f32[32]{0:T(128)S(1)} %convolution_bitcast_fusion.10, f32[32,224]{1,0:T(8,128)} %concatenate.176, f32[96,13824]{1,0:T(8,128)} %bitcast.374, f32[96,13824]{1,0:T(8,128)} %bitcast.373), kind=kOutput, calls=%fused_computation.416 | convolution fusion | flops 1197490176 | bytes 14240000 | tf_op jit(solution)/shard_map/dot_general | solution.py:134
  276.9 5.2 broadcast_multiply_fusion.5
  282.1 11.5 %psum.54 = f32[32]{0:T(128)S(1)} all-reduce(f32[32]{0:T(128)S(1)} %broadcast_multiply_fusion.11), channel_id=1, replica_groups=mesh['space'=16,'vel'=8] {'vel'}, use_global_device_ids=true, to_apply=%region_12.15 | all-reduce | flops 32 | bytes 256 | tf_op jit(solution)/shard_map/psum | solution.py:242
  293.8 11.6 %fusion.291 = (f32[32]{0:T(128)S(1)}, f32[32,13824]{1,0:T(8,128)}) fusion(f32[32,13824]{1,0:T(8,128)} %copy-done.20, f32[13824]{0:T(1024)} %fusion.118, f32[32]{0:T(128)S(1)} %convolution_bitcast_fusion.9, f32[32,224]{1,0:T(8,128)S(1)} %copy-done.32, f32[96,13824]{1,0:T(8,128)} %bitcast.376, f32[96,13824]{1,0:T(8,128)} %bitcast.375), kind=kOutput, calls=%fused_computation.417 | convolution fusion | flops 1197490176 | bytes 14240000 | tf_op jit(solution)/shard_map/dot_general | solution.py:134
  305.3 12.4 %psum.55 = f32[32]{0:T(128)S(1)} all-reduce(f32[32]{0:T(128)S(1)} %broadcast_multiply_fusion.10), channel_id=1, replica_groups=mesh['space'=16,'vel'=8] {'vel'}, use_global_device_ids=true, to_apply=%region_14.17 | all-reduce | flops 32 | bytes 256 | tf_op jit(solution)/shard_map/psum | solution.py:242
  318.0 2.8 broadcast_multiply_fusion.3
  320.8 7.3 %fusion.1 = f32[32,13824]{1,0:T(8,128)S(1)} fusion(f32[32,13824]{1,0:T(8,128)S(1)} %copy-done.19, f32[32,224]{1,0:T(8,128)S(1)} %copy-done.33, f32[96,13824]{1,0:T(8,128)S(1)} %bitcast.378, f32[96,13824]{1,0:T(8,128)S(1)} %bitcast.377, f32[32]{0:T(128)S(1)} %convolution_bitcast_fusion.8, f32[13824]{0:T(1024)S(1)} %copy-done.29), kind=kOutput, calls=%fused_computation.2 | convolution fusion | flops 1197047808 | bytes 14239872 | tf_op jit(solution)/shard_map/dot_general | solution.py:134
  329.4 2.0 fusion.57
  331.4 14.8 %all-gather.2 = f32[256,34]{1,0:T(8,128)} all-gather(f32[32,34]{1,0:T(8,128)S(1)} %fusion.57), channel_id=4, replica_groups=mesh['space'=16,'vel'=8] {'vel'}, dimensions={0}, use_global_device_ids=true | all-gather | bytes 39168 | tf_op jit(solution)/shard_map/all_gather | solution.py:16
  347.3 2.9 cholesky.107
  351.6 2.4 custom-call.11
  354.3 3.1 fusion.298
  357.4 2.5 broadcast_multiply_fusion.1
  360.2 10.9 %fusion.51 = f32[32,224]{1,0:T(8,128)S(1)} fusion(f32[32,13824]{1,0:T(8,128)S(1)} %fusion.298, f32[32,13824]{1,0:T(8,128)S(1)} %copy-done.5, f32[96,13824]{1,0:T(8,128)S(1)} %bitcast.372, f32[96,13824]{1,0:T(8,128)S(1)} %bitcast.371), kind=kOutput, calls=%fused_computation.73 | convolution fusion | flops 1195285504 | bytes 14184448 | tf_op jit(solution)/shard_map/dot_general | solution.py:66
  371.2 13.1 %all-gather.3 = f32[256,224]{1,0:T(8,128)S(1)} all-gather(f32[32,224]{1,0:T(8,128)S(1)} %fusion.51), channel_id=5, replica_groups=mesh['space'=16,'vel'=8] {'vel'}, dimensions={0}, use_global_device_ids=true | all-gather | bytes 258048 | tf_op jit(solution)/shard_map/all_gather | solution.py:16
  384.3 5.4 collective-permute-start.2
  393.4 2.7 collective-permute-done.2
  396.9 7.3 %fusion.38 = f32[32,8192]{1,0:T(8,128)S(1)} fusion(f32[32,8192]{1,0:T(8,128)S(1)} %fusion.293, f32[24,8,64,128]{3,2,1,0:T(8,128)S(1)} %bitcast.368, f32[8192]{0:T(1024)S(1)} %bitcast.401, f32[32]{0:T(128)S(1)} %copy-done.34, f32[8192]{0:T(1024)S(1)} %bitcast.391, f32[32,224]{1,0:T(8,128)S(1)} %reduce_sum.74), kind=kOutput, calls=%fused_computation.44 | convolution fusion | flops 605552640 | bytes 8482944 | tf_op jit(solution)/shard_map/dot_general | solution.py:125
  405.6 6.2 collective-permute-start.4
  412.4 4.8 collective-permute-done.3
  418.6 7.3 %fusion.36 = f32[32,8192]{1,0:T(8,128)S(1)} fusion(f32[32,8192]{1,0:T(8,128)S(1)} %fusion.38, f32[24,8,64,128]{3,2,1,0:T(8,128)S(1)} %bitcast.369, f32[8192]{0:T(1024)S(1)} %bitcast.402, f32[32]{0:T(128)S(1)} %copy-done.34, f32[8192]{0:T(1024)S(1)} %bitcast.392, f32[32,224]{1,0:T(8,128)S(1)} %reduce_sum.74), kind=kOutput, calls=%fused_computation.41 | convolution fusion | flops 605552640 | bytes 8482944 | tf_op jit(solution)/shard_map/dot_general | solution.py:125
  427.4 5.6 collective-permute-start.6
  433.6 4.2 collective-permute-done.5
  439.2 7.2 %fusion.34 = f32[32,8192]{1,0:T(8,128)S(1)} fusion(f32[32,8192]{1,0:T(8,128)S(1)} %fusion.36, f32[24,8,64,128]{3,2,1,0:T(8,128)S(1)} %bitcast.370, f32[8192]{0:T(1024)S(1)} %bitcast.400, f32[32]{0:T(128)S(1)} %copy-done.34, f32[8192]{0:T(1024)S(1)} %bitcast.393, f32[32,224]{1,0:T(8,128)S(1)} %reduce_sum.74), kind=kOutput, calls=%fused_computation.38 | convolution fusion | flops 605552640 | bytes 8482944 | tf_op jit(solution)/shard_map/dot_general | solution.py:125
  447.4 74.4 %psum.51 = f32[32,32]{0,1:T(8,128)S(1)} all-reduce(f32[32,32]{0,1:T(8,128)S(1)} %convolution_multiply_fusion.2), channel_id=1, replica_groups=mesh['space'=16,'vel'=8] {'space'}, use_global_device_ids=true, to_apply=%region_7.10 | all-reduce | flops 1024 | bytes 8192 | tf_op jit(solution)/shard_map/psum | solution.py:162
  521.9 2.9 cholesky.96
  526.2 2.4 custom-call.10
  531.4 9.2 %collective-permute-done.7 = f32[32,1,16,128]{3,2,1,0:T(8,128)S(1)} collective-permute-done((f32[32,1,16,128]{3,2,1,0:T(8,128)S(1)}, f32[32,1,16,128]{3,2,1,0:T(8,128)S(1)}, u32[]{:S(2)}, u32[]{:S(2)}) %collective-permute-start.7) | collective-permute-done | bytes 262176 | tf_op jit(solution)/shard_map/ppermute | solution.py:26
  543.6 4.9 convolution_multiply_fusion
  548.5 69.5 %psum.52 = f32[32,160]{1,0:T(8,128)S(1)} all-reduce(f32[32,160]{1,0:T(8,128)S(1)} %convolution_multiply_fusion), channel_id=1, replica_groups=mesh['space'=16,'vel'=8] {'space'}, use_global_device_ids=true, to_apply=%region_8.11 | all-reduce | flops 5120 | bytes 40960 | tf_op jit(solution)/shard_map/psum | solution.py:162
  (258 shorter events, 64.7 us)
Async XLA Ops:
  0.6 236.4 %copy-start = (f32[32,32]{1,0:T(8,128)S(1)}, f32[32,32]{1,0:T(8,128)}, u32[]{:S(2)}) copy-start(f32[32,32]{1,0:T(8,128)} %param.8) | copy-start | bytes 12292
  2.3 154.9 %collective-permute-start = (f32[32,1,16,128]{3,2,1,0:T(8,128)}, f32[32,1,16,128]{3,2,1,0:T(8,128)}, u32[]{:S(2)}, u32[]{:S(2)}) collective-permute-start(f32[32,1,16,128]{3,2,1,0:T(8,128)} %slice.264), channel_id=1, source_target_pairs={{120,0},{0,8},{8,16},{16,24},{24,32},{32,40},{40,48},{48,56},{56,6... | collective-permute-start | bytes 786440 | tf_op jit(solution)/shard_map/ppermute | solution.py:26
  87.7 3.0 copy-start.25
  96.2 0.6 copy-start.30
  96.8 17.3 %copy-start.36 = (f32[34]{0:T(128)}, f32[34]{0:T(128)S(1)}, u32[]{:S(2)}) copy-start(f32[34]{0:T(128)S(1)} %pad.64.clone) | copy-start | bytes 412
  124.5 5.3 copy-start.3
  128.6 30.3 %copy-start.7 = (f32[3,13824]{1,0:T(4,128)}, f32[3,13824]{1,0:T(4,128)S(1)}, u32[]{:S(2)}) copy-start(f32[3,13824]{1,0:T(4,128)S(1)} %get-tuple-element.50) | copy-start | bytes 497668
  128.6 1.6 copy-start.17
  130.2 27.0 %copy-start.26 = (f32[32,32]{1,0:T(8,128)S(1)}, f32[32,32]{1,0:T(8,128)}, u32[]{:S(2)}) copy-start(f32[32,32]{1,0:T(8,128)} %copy-done.25) | copy-start | bytes 12292
  155.3 4.9 copy-start.10
  156.4 3.2 copy-start.11
  158.7 2.1 copy-start.23
  158.9 2.1 copy-start.6
  160.9 76.5 %copy-start.4 = (f32[32,13824]{1,0:T(8,128)S(1)}, f32[32,13824]{1,0:T(8,128)}, u32[]{:S(2)}) copy-start(f32[32,13824]{1,0:T(8,128)} %copy-done.3) | copy-start | bytes 5308420
  236.3 22.2 %copy-start.21 = (f32[32,160]{1,0:T(8,128)}, f32[32,160]{1,0:T(8,128)S(1)}, u32[]{:S(2)}) copy-start(f32[32,160]{1,0:T(8,128)S(1)} %psum.50) | copy-start | bytes 61444
  244.0 4.3 copy-start.28
  258.7 6.7 %slice-start = ((f32[32,160]{1,0:T(8,128)}), f32[32,96]{1,0:T(8,128)S(1)}, s32[]{:S(2)}) async-start(f32[32,160]{1,0:T(8,128)} %copy-done.21), calls=%async_computation | async-start | bytes 32768 | tf_op jit(solution)/shard_map/slice | solution.py:102
  258.7 6.7 %copy-start.27 = (f32[32,32]{1,0:T(8,128)S(1)}, f32[32,32]{1,0:T(8,128)}, u32[]{:S(2)}) copy-start(f32[32,32]{1,0:T(8,128)} %get-tuple-element.51) | copy-start | bytes 12292
  266.2 10.7 %copy-start.8 = (f32[3,13824]{1,0:T(4,128)S(1)}, f32[3,13824]{1,0:T(4,128)}, u32[]{:S(2)}) copy-start(f32[3,13824]{1,0:T(4,128)} %copy-done.7) | copy-start | bytes 497668
  276.8 5.2 copy-start.20
  276.9 16.7 %copy-start.22 = (f32[32,160]{1,0:T(8,128)S(1)}, f32[32,160]{1,0:T(8,128)}, u32[]{:S(2)}) copy-start(f32[32,160]{1,0:T(8,128)} %copy-done.21) | copy-start | bytes 61444
  276.9 16.9 %copy-start.32 = (f32[32,224]{1,0:T(8,128)S(1)}, f32[32,224]{1,0:T(8,128)}, u32[]{:S(2)}) copy-start(f32[32,224]{1,0:T(8,128)} %concatenate.176) | copy-start | bytes 86020
  318.0 2.8 copy-start.19
  318.0 2.8 copy-start.29
  318.0 2.8 copy-start.33
  320.8 8.6 %copy-start.31 = (f32[1,13824]{1,0:T(1,128)S(1)}, f32[1,13824]{1,0:T(1,128)}, u32[]{:S(2)}) copy-start(f32[1,13824]{1,0:T(1,128)} %copy-done.30) | copy-start | bytes 165892
  320.8 8.6 %copy-start.37 = (f32[34]{0:T(128)S(1)}, f32[34]{0:T(128)}, u32[]{:S(2)}) copy-start(f32[34]{0:T(128)} %copy-done.36) | copy-start | bytes 412
  328.1 1.2 copy-start.18
  357.3 2.9 copy-start.9
  357.4 2.9 copy-start.5
  359.9 30.5 %collective-permute-start.1 = (f32[32,1,16,128]{3,2,1,0:T(8,128)}, f32[32,1,16,128]{3,2,1,0:T(8,128)}, u32[]{:S(2)}, u32[]{:S(2)}) collective-permute-start(f32[32,1,16,128]{3,2,1,0:T(8,128)} %get-tuple-element.48), channel_id=1, source_target_pairs={{0,8},{8,16},{16,24},{24,32},{32,40},{40,48},{48,56},{56,64},{64,7... | collective-permute-start | bytes 786440 | tf_op jit(solution)/shard_map/ppermute | solution.py:36
  360.2 29.5 %copy-start.35 = (f32[32,1]{0,1:T(1,128)S(1)}, f32[32,1]{0,1:T(1,128)}, u32[]{:S(2)}) copy-start(f32[32,1]{0,1:T(1,128)} %convolution_bitcast_fusion.11) | copy-start | bytes 388
  384.3 8.7 %copy-start.15 = (f32[32,4,16,127]{3,2,1,0:T(8,128)S(1)}, f32[32,4,16,127]{3,2,1,0:T(8,128)}, u32[]{:S(2)}) copy-start(f32[32,4,16,127]{3,2,1,0:T(8,128)} %get-tuple-element.40) | copy-start | bytes 3121156
  384.3 8.7 %copy-start.16 = (f32[32,4,16,1]{3,2,1,0:T(8,128)S(1)}, f32[32,4,16,1]{3,2,1,0:T(8,128)}, u32[]{:S(2)}) copy-start(f32[32,4,16,1]{3,2,1,0:T(8,128)} %get-tuple-element.42) | copy-start | bytes 24580
  384.3 11.8 %collective-permute-start.2 = (f32[32,1,16,128]{3,2,1,0:T(8,128)}, f32[32,1,16,128]{3,2,1,0:T(8,128)S(1)}, u32[]{:S(2)}, u32[]{:S(2)}) collective-permute-start(f32[32,1,16,128]{3,2,1,0:T(8,128)} %get-tuple-element.47), channel_id=1, source_target_pairs={{8,0},{16,8},{24,16},{32,24},{40,32},{48,40},{56,48},{64,56},{72,6... | collective-permute-start | bytes 786440 | tf_op jit(solution)/shard_map/ppermute | solution.py:38
  391.4 4.8 copy-start.12
  391.4 4.8 copy-start.24
  392.9 3.5 copy-start.13
  393.0 3.5 copy-start.14
  393.4 3.5 copy-start.34
  405.5 11.7 %collective-permute-start.3 = (f32[32,1,16,128]{3,2,1,0:T(8,128)S(1)}, f32[32,1,16,128]{3,2,1,0:T(8,128)S(1)}, u32[]{:S(2)}, u32[]{:S(2)}) collective-permute-start(f32[32,1,16,128]{3,2,1,0:T(8,128)S(1)} %get-tuple-element.38), channel_id=1, source_target_pairs={{0,8},{8,16},{16,24},{24,32},{32,40},{40,48},{48,56},{56,64},{64,7... | collective-permute-start | bytes 786440 | tf_op jit(solution)/shard_map/ppermute | solution.py:36
  405.6 12.3 %collective-permute-start.4 = (f32[32,1,16,128]{3,2,1,0:T(8,128)S(1)}, f32[32,1,16,128]{3,2,1,0:T(8,128)S(1)}, u32[]{:S(2)}, u32[]{:S(2)}) collective-permute-start(f32[32,1,16,128]{3,2,1,0:T(8,128)S(1)} %get-tuple-element.37), channel_id=1, source_target_pairs={{8,0},{16,8},{24,16},{32,24},{40,32},{48,40},{56,48},{64,56},{72,6... | collective-permute-start | bytes 786440 | tf_op jit(solution)/shard_map/ppermute | solution.py:38
  427.2 10.5 %collective-permute-start.5 = (f32[32,1,16,128]{3,2,1,0:T(8,128)S(1)}, f32[32,1,16,128]{3,2,1,0:T(8,128)S(1)}, u32[]{:S(2)}, u32[]{:S(2)}) collective-permute-start(f32[32,1,16,128]{3,2,1,0:T(8,128)S(1)} %get-tuple-element.28), channel_id=1, source_target_pairs={{0,8},{8,16},{16,24},{24,32},{32,40},{40,48},{48,56},{56,64},{64,7... | collective-permute-start | bytes 786440 | tf_op jit(solution)/shard_map/ppermute | solution.py:36
  427.4 11.1 %collective-permute-start.6 = (f32[32,1,16,128]{3,2,1,0:T(8,128)S(1)}, f32[32,1,16,128]{3,2,1,0:T(8,128)S(1)}, u32[]{:S(2)}, u32[]{:S(2)}) collective-permute-start(f32[32,1,16,128]{3,2,1,0:T(8,128)S(1)} %get-tuple-element.27), channel_id=1, source_target_pairs={{8,0},{16,8},{24,16},{32,24},{40,32},{48,40},{56,48},{64,56},{72,6... | collective-permute-start | bytes 786440 | tf_op jit(solution)/shard_map/ppermute | solution.py:38
  530.1 1.3 copy-start.2
  530.8 9.8 %collective-permute-start.7 = (f32[32,1,16,128]{3,2,1,0:T(8,128)S(1)}, f32[32,1,16,128]{3,2,1,0:T(8,128)S(1)}, u32[]{:S(2)}, u32[]{:S(2)}) collective-permute-start(f32[32,1,16,128]{3,2,1,0:T(8,128)S(1)} %slice.379), channel_id=1, source_target_pairs={{120,0},{0,8},{8,16},{16,24},{24,32},{32,40},{40,48},{48,56},{56,6... | collective-permute-start | bytes 786440 | tf_op jit(solution)/shard_map/ppermute | solution.py:26
  543.4 84.5 %copy-start.1 = (f32[32,32]{1,0:T(8,128)S(1)}, f32[32,32]{1,0:T(8,128)}, u32[]{:S(2)}) copy-start(f32[32,32]{1,0:T(8,128)} %param.8) | copy-start | bytes 12292
